TPU v7x, 32 devices: a whole 2x2x4 slice. The times are simulated.
32 devices in a mesh: grp: 2 (over y), seq: 4 (over z), head: 2 (over x), sub: 2 (over core).
Axes of the slice: x: 2, y: 2, z: 4, core: 2. Of those that a mesh axis runs over, the one named last changes fastest.
Arguments:
- queries: float32 [1536, 2048], P(('grp', 'seq'), ('head', 'sub')), parts along dimension 0, may hold values from -6 to 6
- keys: float32 [1536, 2048], P(('grp', 'seq'), ('head', 'sub')), parts along dimension 0, may hold values from -6 to 6
- values: float32 [1536, 2048], P(('grp', 'seq'), ('head', 'sub')), parts along dimension 0, may hold values from -40 to 40
- opt_queries: float32 [16, 64, 2048], P(('grp', 'seq'), None, ('head', 'sub')), parts along dimension 0, may hold values from -6 to 6
- opt_keys: float32 [16, 64, 2048], P(('grp', 'seq'), None, ('head', 'sub')), parts along dimension 0, may hold values from -6 to 6
- opt_values: float32 [16, 64, 2048], P(('grp', 'seq'), None, ('head', 'sub')), parts along dimension 0, may hold values from -40 to 40
- opt_offsets: int32 [16], P(('grp', 'seq')), parts along dimension 0, may hold values from 0 to 192
- opt_lengths: int32 [16], P(('grp', 'seq')), parts along dimension 0, may hold values from 1 to 64, 320 in all
- norm_gain: float32 [2048], P(('head', 'sub')), may hold values from 0.5 to 2
- out_weight: bfloat16 [2048, 4096], P(('head', 'sub')), may hold values from -0.125 to 0.125
Outputs:
- ctx_out: bfloat16 [1536, 4096], P(('grp', 'seq'), ('head', 'sub')), parts along dimension 0
- opt_out: bfloat16 [16, 64, 4096], P(('grp', 'seq'), None, ('head', 'sub')), parts along dimension 0
There are 2 independent parts, one for each index of `grp`. A program takes and returns all parts, laid end to end along the dimension named above; an argument that names none is the same for every part. Nothing has to cross between parts.
Inputs may be any that keep to these rules, and one draw needn't show every extreme that they name: `opt_lengths`: within each scoring group the 8 lengths sum to 320, and the longest option of each group has exactly 64 tokens in every draw.
All inputs are finite; a program needn't handle non-finite values.
Results may differ from a plain program's by a relative error of at most 0.017.
Values may be sent and summed in bfloat16 or wider, within the bound.
A program may use at most 64 MiB of HBM per device.

v0:
```python
import jax
import jax.numpy as jnp
from jax import lax
from jax.sharding import PartitionSpec as P

DH = 128


norm_epsilon = 1e-05


def entering(value, axis, join, neutral):
    place = lax.axis_index(axis)
    gathered = lax.all_gather(value.astype(jnp.bfloat16), axis)
    state = jnp.zeros_like(value) + jnp.asarray(neutral, value.dtype)

    def one(hop, state):
        return join(state, lax.dynamic_index_in_dim(gathered, hop, 0, False).astype(value.dtype))

    return lax.fori_loop(0, place, one, state)


def head_norm(attended, gain, mask):
    mean_square = jnp.mean(attended * attended, axis=-1, keepdims=True)
    return (attended * lax.rsqrt(mean_square + norm_epsilon) * gain * mask).astype(jnp.bfloat16)


def combine_sum(earlier, later):
    return earlier + later


def grouped_project(rows, weight_columns, groups):
    count = rows.shape[0]
    flat = rows.reshape(count, groups, rows.shape[1] // groups)
    weight_groups = weight_columns.reshape(
        groups, weight_columns.shape[0] // groups, weight_columns.shape[1]
    )
    partial_value = jnp.einsum(
        "rgk,gkd->grd", flat, weight_groups, preferred_element_type=jnp.float32
    )
    partial_value = lax.optimization_barrier(partial_value.astype(jnp.bfloat16)).astype(jnp.float32)
    return jnp.sum(partial_value, axis=0).astype(jnp.bfloat16)


def on_device(
    queries,
    keys,
    values,
    opt_queries,
    opt_keys,
    opt_values,
    opt_offsets,
    opt_lengths,
    norm_gain,
    out_weight,
):
    highest = lax.Precision.HIGHEST
    tok_rows = queries.shape[0]
    heads = queries.shape[1] // DH
    opt_count = opt_queries.shape[0]
    slot_count = opt_queries.shape[1]
    group_count = lax.axis_size(("head", "sub"))
    weight_columns = lax.all_to_all(
        out_weight, ("head", "sub"), split_axis=1, concat_axis=0, tiled=True
    )
    block_q = queries.reshape(tok_rows, heads, DH)
    block_k = keys.reshape(tok_rows, heads, DH)
    block_v = values.reshape(tok_rows, heads, DH)
    gain = norm_gain.reshape(heads, DH)
    states = jnp.einsum("thd,the->hde", block_k, block_v, precision=highest)
    positions = jnp.arange(tok_rows, dtype=jnp.int32)
    causal = (positions[:, None] >= positions[None, :]).astype(jnp.float32)
    scores = jnp.einsum("thd,shd->hts", block_q, block_k, precision=highest) * causal[None]
    intra = jnp.einsum("hts,she->the", scores, block_v, precision=highest)
    opt_q = opt_queries.reshape(opt_count, slot_count, heads, DH)
    opt_k = opt_keys.reshape(opt_count, slot_count, heads, DH)
    opt_v = opt_values.reshape(opt_count, slot_count, heads, DH)
    before = (positions[None, :] < opt_offsets[:, None]).astype(jnp.float32)
    local = jnp.einsum("ot,thd,the->ohde", before, block_k, block_v, precision=highest)
    slots = jnp.arange(slot_count, dtype=jnp.int32)
    slot_causal = (slots[:, None] >= slots[None, :]).astype(jnp.float32)
    opt_scores = (
        jnp.einsum("oihd,ojhd->ohij", opt_q, opt_k, precision=highest) * slot_causal[None, None]
    )
    opt_intra = jnp.einsum("ohij,ojhe->oihe", opt_scores, opt_v, precision=highest)
    prefix = entering(states, "seq", combine_sum, jnp.zeros_like(states))
    inter = jnp.einsum("thd,hde->the", block_q, prefix, precision=highest)
    context_normed = head_norm(inter + intra, gain, 1.0).reshape(tok_rows, heads * DH)
    opt_state = prefix[None] + local
    opt_inter = jnp.einsum("oihd,ohde->oihe", opt_q, opt_state, precision=highest)
    valid = (slots[None, :] < opt_lengths[:, None]).astype(jnp.float32)
    opt_normed = head_norm(opt_inter + opt_intra, gain, valid[:, :, None, None]).reshape(
        opt_count * slot_count, heads * DH
    )
    gathered_ctx, gathered_opt = (
        lax.all_gather(context_normed, ("head", "sub"), axis=1, tiled=True),
        lax.all_gather(opt_normed, ("head", "sub"), axis=1, tiled=True),
    )
    context_out = grouped_project(gathered_ctx, weight_columns, group_count)
    opt_rows = grouped_project(gathered_opt, weight_columns, group_count)
    option_out = opt_rows.reshape(opt_count, slot_count, opt_rows.shape[1])
    return (context_out, option_out)


def solution(mesh):
    placed = (
        P(("grp", "seq"), ("head", "sub")),
        P(("grp", "seq"), ("head", "sub")),
        P(("grp", "seq"), ("head", "sub")),
        P(("grp", "seq"), None, ("head", "sub")),
        P(("grp", "seq"), None, ("head", "sub")),
        P(("grp", "seq"), None, ("head", "sub")),
        P(("grp", "seq")),
        P(("grp", "seq")),
        P(("head", "sub")),
        P(("head", "sub"), None),
    )
    return jax.shard_map(
        on_device,
        mesh=mesh,
        in_specs=placed,
        out_specs=(P(("grp", "seq"), ("head", "sub")), P(("grp", "seq"), None, ("head", "sub"))),
        check_vma=False,
    )
```

profile of v0, /device:TPU:25, one launch (start us, length us, event | category | flops | bytes accessed | tf_op | source)
XLA Modules:
  0.0 91.3 jit_solution(10964770409362976219)
XLA Ops:
  0.6 0.0 copy-start
  0.6 6.5 %copy.40 = bf16[512,4096]{0,1:T(8,128)(2,1)} copy(bf16[512,4096]{1,0:T(8,128)(2,1)} %param.21) | data formatting | bytes 8388608 | tf_op args[9]
  7.2 6.3 %copy.41 = bf16[512,4,1024]{2,0,1:T(8,128)(2,1)} copy(bf16[512,4,1024]{0,2,1:T(8,128)(2,1)} %bitcast.132) | data formatting | bytes 8388608 | tf_op jit(solution)/shard_map/all_to_all | solution.py:63
  13.5 0.0 copy-start.1
  13.5 5.6 %all-to-all-start = ((bf16[512,4,1024]{2,0,1:T(8,128)(2,1)}), bf16[512,4,1024]{2,0,1:T(8,128)(2,1)}, u32[]{:S(2)}, u32[]{:S(2)}) async-start(bf16[512,4,1024]{2,0,1:T(8,128)(2,1)} %copy.41), calls=%async_computation | async-start | bytes 8388608 | tf_op jit(solution)/shard_map/all_to_all | solution.py:63
  19.1 0.0 copy-start.8
  19.1 0.0 copy-start.4
  19.1 0.0 copy-start.5
  19.1 0.0 copy-start.9
  19.1 0.0 copy-done
  19.2 0.0 copy-done.1
  19.2 0.0 copy-start.6
  19.2 1.1 %convolution_convert_fusion = bf16[4,128,128]{2,1,0:T(8,128)(2,1)S(1)} fusion(f32[192,512]{1,0:T(8,128)S(1)} %copy-done.1, f32[192,512]{1,0:T(8,128)S(1)} %copy-done), kind=kOutput, calls=%fused_computation.17 | convolution fusion | flops 151060480 | bytes 917504 | tf_op jit(solution)/shard_map/thd,the->hde/dot_general | solution.py:70
  20.3 13.0 %all-gather = bf16[16,128,128]{2,1,0:T(8,128)(2,1)S(1)} all-gather(bf16[4,128,128]{2,1,0:T(8,128)(2,1)S(1)} %convolution_convert_fusion), channel_id=2, replica_groups=mesh['grp'=2,'seq'=4,'head'=2,'sub'=2] {'seq'}, dimensions={0}, use_global_device_ids=true | all-gather | bytes 655360 | tf_op jit(solution)/shard_map/all_gather | solution.py:14
  33.3 0.0 copy-start.7
  33.3 0.2 while.10
  33.5 0.0 copy-done.8
  33.6 0.0 copy-start.3
  33.6 0.1 fusion.39
  33.6 0.0 copy-done.4
  33.6 0.0 copy-done.5
  33.6 0.5 convolution_multiply_fusion.1
  34.2 0.0 copy-done.9
  34.2 0.1 compare_convert_fusion.1
  34.3 1.9 %fusion.10 = f32[2,4,128,128]{3,2,1,0:T(8,128)S(1)} fusion(f32[192,4,128]{2,0,1:T(8,128)S(1)} %copy_bitcast_fusion, f32[192,2]{0,1:T(2,128)S(1)} %fusion.39, f32[4,128,128]{2,1,0:T(8,128)S(1)} %get-tuple-element.25, f32[192,512]{1,0:T(8,128)S(1)} %copy-done.1), kind=kOutput, calls=%fused_computation.9 | convolution fusion | flops 302317568 | bytes 1574400 | tf_op jit(solution)/shard_map/ot,thd,the->ohde/dot_general | solution.py:79
  36.2 0.6 convolution_bitcast_fusion.3
  36.8 0.0 copy-done.6
  36.8 0.5 multiply_reduce_fusion.1
  37.3 0.0 copy-done.7
  37.3 0.2 multiply_convert_fusion.1
  37.5 0.1 copy.49
  37.6 33.1 %all_gather.15 = bf16[128,2048]{1,0:T(8,128)(2,1)S(1)} all-gather(bf16[128,512]{1,0:T(8,128)(2,1)S(1)} %bitcast.136), channel_id=1, replica_groups=mesh['grp'=2,'seq'=4,'head'=2,'sub'=2] {'head','sub'}, dimensions={1}, use_global_device_ids=true | all-gather | bytes 655360 | tf_op jit(solution)/shard_map/all_gather | solution.py:97
  70.8 1.0 %copy.50 = bf16[128,2048]{0,1:T(8,128)(2,1)} copy(bf16[128,2048]{1,0:T(8,128)(2,1)S(1)} %all_gather.15) | data formatting | bytes 1048576 | tf_op jit(solution)/shard_map/all_gather | solution.py:97
  71.8 0.0 copy-done.3
  71.8 0.5 convolution_bitcast_fusion.1
  72.3 0.8 convolution_multiply_fusion
  73.1 1.0 %multiply_reduce_fusion = (f32[192,4]{0,1:T(4,128)S(1)}, f32[192,4,128]{2,0,1:T(8,128)S(1)}) fusion(f32[192,4,128]{2,0,1:T(8,128)S(1)} %convolution_bitcast_fusion.1, f32[4,192,192]{2,1,0:T(8,128)S(1)} %convolution_multiply_fusion, f32[192,512]{1,0:T(8,128)S(1)} %copy-done.1), kind=kOutput, calls=%fused_computation.31 | convolution fusion | flops 226786560 | bytes 1772544 | tf_op jit(solution)/shard_map/hts,she->the/dot_general | solution.py:74
  74.1 0.2 copy_bitcast_fusion.1
  74.3 8.7 %all_gather.14 = bf16[192,2048]{1,0:T(8,128)(2,1)S(1)} all-gather(bf16[192,512]{1,0:T(8,128)(2,1)S(1)} %copy_bitcast_fusion.1), channel_id=1, replica_groups=mesh['grp'=2,'seq'=4,'head'=2,'sub'=2] {'head','sub'}, dimensions={1}, use_global_device_ids=true | all-gather | bytes 983040 | tf_op jit(solution)/shard_map/all_gather | solution.py:96
  83.0 0.0 all-to-all-done
  83.0 0.0 copy-start.2
  83.0 3.2 %fusion.4 = bf16[4,192,1024]{2,1,0:T(8,128)(2,1)S(1)} fusion(bf16[512,4,1024]{2,0,1:T(8,128)(2,1)} %all-to-all-done, bf16[24,4,8,512]{3,2,1,0:T(8,128)(2,1)S(1)} %bitcast.133), kind=kOutput, calls=%fused_computation.5 | convolution fusion | flops 806092800 | bytes 6553600 | tf_op jit(solution)/shard_map/rgk,gkd->grd/dot_general | solution.py:38
  86.3 0.0 copy-done.2
  86.3 3.0 %fusion.7 = bf16[4,128,1024]{2,1,0:T(8,128)(2,1)S(1)} fusion(bf16[128,4,512]{0,2,1:T(8,128)(2,1)S(1)} %bitcast.134, bf16[512,4,1024]{2,0,1:T(8,128)(2,1)} %all-to-all-done), kind=kOutput, calls=%fused_computation.6 | convolution fusion | flops 537395200 | bytes 5767168 | tf_op jit(solution)/shard_map/rgk,gkd->grd/dot_general | solution.py:38
  89.3 1.1 %reduce_sum.43 = bf16[192,1024]{1,0:T(8,128)(2,1)} reduce(bf16[4,192,1024]{2,1,0:T(8,128)(2,1)S(1)} %fusion.4, bf16[]{:T(256)} %constant.28.clone.1), dimensions={0}, to_apply=%region_3.4 | reduce | flops 589824 | bytes 1966082 | tf_op jit(solution)/shard_map/reduce_sum | solution.py:42
  90.4 0.9 %reduce_sum.45 = bf16[128,1024]{1,0:T(8,128)(2,1)} reduce(bf16[4,128,1024]{2,1,0:T(8,128)(2,1)S(1)} %fusion.7, bf16[]{:T(256)} %constant.28.clone.1), dimensions={0}, to_apply=%region_5.6 | reduce | flops 393216 | bytes 1310722 | tf_op jit(solution)/shard_map/reduce_sum | solution.py:42
  (10 shorter events, 0.2 us)
Async XLA Ops:
  0.6 18.5 %copy-start = (f32[192,512]{1,0:T(8,128)S(1)}, f32[192,512]{1,0:T(8,128)}, u32[]{:S(2)}) copy-start(f32[192,512]{1,0:T(8,128)} %param.13) | copy-start | bytes 1179652
  13.5 5.7 %copy-start.1 = (f32[192,512]{1,0:T(8,128)S(1)}, f32[192,512]{1,0:T(8,128)}, u32[]{:S(2)}) copy-start(f32[192,512]{1,0:T(8,128)} %param.14) | copy-start | bytes 1179652
  13.5 69.5 %all-to-all-start = ((bf16[512,4,1024]{2,0,1:T(8,128)(2,1)}), bf16[512,4,1024]{2,0,1:T(8,128)(2,1)}, u32[]{:S(2)}, u32[]{:S(2)}) async-start(bf16[512,4,1024]{2,0,1:T(8,128)(2,1)} %copy.41), calls=%async_computation | async-start | bytes 8388608 | tf_op jit(solution)/shard_map/all_to_all | solution.py:63
  19.1 14.4 %copy-start.8 = (s32[2]{0:T(128)S(1)}, s32[2]{0:T(128)}, u32[]{:S(2)}) copy-start(s32[2]{0:T(128)} %param.18) | copy-start | bytes 28
  19.1 14.5 %copy-start.4 = (f32[2,64,512]{2,1,0:T(8,128)S(1)}, f32[2,64,512]{2,1,0:T(8,128)}, u32[]{:S(2)}) copy-start(f32[2,64,512]{2,1,0:T(8,128)} %param.15) | copy-start | bytes 786436
  19.1 14.5 %copy-start.5 = (f32[2,64,512]{2,1,0:T(8,128)S(1)}, f32[2,64,512]{2,1,0:T(8,128)}, u32[]{:S(2)}) copy-start(f32[2,64,512]{2,1,0:T(8,128)} %param.16) | copy-start | bytes 786436
  19.1 15.1 %copy-start.9 = (s32[2]{0:T(128)S(1)}, s32[2]{0:T(128)}, u32[]{:S(2)}) copy-start(s32[2]{0:T(128)} %param.19) | copy-start | bytes 28
  19.2 17.6 %copy-start.6 = (f32[2,64,512]{2,1,0:T(8,128)S(1)}, f32[2,64,512]{2,1,0:T(8,128)}, u32[]{:S(2)}) copy-start(f32[2,64,512]{2,1,0:T(8,128)} %param.17) | copy-start | bytes 786436
  33.3 4.0 %copy-start.7 = (f32[512]{0:T(512)S(1)}, f32[512]{0:T(512)}, u32[]{:S(2)}) copy-start(f32[512]{0:T(512)} %param.20) | copy-start | bytes 6148
  33.6 38.3 %copy-start.3 = (f32[192,512]{1,0:T(8,128)S(1)}, f32[192,512]{1,0:T(8,128)}, u32[]{:S(2)}) copy-start(f32[192,512]{1,0:T(8,128)} %param.12) | copy-start | bytes 1179652
  83.0 3.2 %copy-start.2 = (bf16[128,2048]{0,1:T(8,128)(2,1)S(1)}, bf16[128,2048]{0,1:T(8,128)(2,1)}, u32[]{:S(2)}) copy-start(bf16[128,2048]{0,1:T(8,128)(2,1)} %copy.50) | copy-start | bytes 1572868
where the time goes:
time: 92 us; the launch traced here: 91.3 us
  blocking collectives  54.9 us (60%)
  local copies, waits for them, and re-layouts  14.1 us (15%)
  matrix products  13.1 us (14%)
  starting transfers between devices  5.6 us (6%)
  other arithmetic  2.7 us (3%)
    all_gather x1, blocking collectives, on_device(): lax.all_gather(opt_normed, ('head', 'sub'), axis=1, tiled=True)  33.1 us
    all_gather x1, blocking collectives, entering(): gathered = lax.all_gather(value.astype(jnp.bfloat16), axis)  13 us
    all_gather x1, blocking collectives, on_device(): lax.all_gather(context_normed, ('head', 'sub'), axis=1, tiled=True)  8.71 us
    unnamed x22, local copies, waits for them, and re-layouts  6.6 us
    all_to_all x1, local copies, waits for them, and re-layouts, on_device(): lax.all_to_all(out_weight, ('head', 'sub'), split_axis=1, concat_axis=0,...  6.33 us
    dot_general x2, matrix products, grouped_project(): jnp.einsum('rgk,gkd->grd', flat, weight_groups, preferred_element_type=jn...  6.22 us
    all_to_all x1, starting transfers between devices, on_device(): lax.all_to_all(out_weight, ('head', 'sub'), split_axis=1, concat_axis=0,...  5.6 us
    reduce_sum x2, other arithmetic, grouped_project(): return jnp.sum(partial_value, axis=0).astype(jnp.bfloat16)  2.06 us
  transfers between devices with their start and end apart: 1, of which 0 were waited for; matrix products, arithmetic and copies ran while one was open for 10% of the time, Pallas kernels for 0%

commit v1 on v0

v1 whole, which is shorter than its diff:
```python
import functools

import jax
import jax.numpy as jnp
from jax import lax
from jax.experimental import pallas as pl
from jax.experimental.pallas import tpu as pltpu
from jax.sharding import PartitionSpec as P

DH = 128
norm_epsilon = 1e-05
MESH = pl.DeviceIdType.MESH
bf16 = jnp.bfloat16
f32 = jnp.float32


def dot(a, b, ca, cb):
    return lax.dot_general(a, b, (((ca,), (cb,)), ((), ())), preferred_element_type=f32)


def kernel(
    sizes,
    q_hbm, k_hbm, v_hbm, oq_hbm, ok_hbm, ov_hbm, offs, lens, gain_ref, w_hbm,
    ctx_out, opt_out,
    q_buf, k_buf, v_buf, state, intra, pre_recv, pre_send, normed, sib_normed,
    w_own, w_sib, part_send, part_recv, own_part,
    in_sem, w_sem, ws_send, ws_recv, pre_ssem, pre_rsem, n_send, n_recv, x_send, x_recv,
):
    n_seq, n_head, n_sub, rows, opts, slots, chunks = sizes
    features = q_hbm.shape[1]
    heads = features // DH
    total = rows + opts * slots
    columns = w_own.shape[2]
    width = columns // chunks
    seq = lax.axis_index("seq")
    head = lax.axis_index("head")
    sub = lax.axis_index("sub")

    barrier = pltpu.get_barrier_semaphore()
    for e in range(1, n_sub):
        pl.semaphore_signal(
            barrier, inc=1, device_id={"sub": lax.rem(sub + e, n_sub)}, device_id_type=MESH
        )
    for d in range(1, n_head):
        pl.semaphore_signal(
            barrier, inc=1, device_id={"head": lax.rem(head + d, n_head)}, device_id_type=MESH
        )

    @pl.when(seq > 0)
    def _():
        pl.semaphore_signal(barrier, inc=1, device_id={"seq": seq - 1}, device_id_type=MESH)

    @pl.when(seq < n_seq - 1)
    def _():
        pl.semaphore_signal(barrier, inc=1, device_id={"seq": seq + 1}, device_id_type=MESH)

    loads = []
    for i, (src, dst, at, count) in enumerate((
        (k_hbm, k_buf, 0, rows),
        (v_hbm, v_buf, 0, rows),
        (q_hbm, q_buf, 0, rows),
        (ok_hbm, k_buf, rows, opts * slots),
        (oq_hbm, q_buf, rows, opts * slots),
        (ov_hbm, v_buf, rows, opts * slots),
    )):
        copy = pltpu.make_async_copy(src, dst.at[pl.ds(at, count)], in_sem.at[i])
        copy.start()
        loads.append(copy)

    def block_of(d, s):
        place = lax.rem(head + d, n_head) * n_sub + s
        return pl.ds(pl.multiple_of(place * columns, columns), columns)

    own_loads = []
    for d in range(n_head):
        copy = pltpu.make_async_copy(w_hbm.at[:, block_of(d, sub)], w_own.at[d], w_sem.at[d])
        own_loads.append(copy)

    def head_cols(h):
        return slice(h * DH, (h + 1) * DH)

    loads[0].wait()
    loads[1].wait()
    for h in range(heads):
        kh = k_buf[:rows, head_cols(h)].astype(bf16)
        vh = v_buf[:rows, head_cols(h)].astype(bf16)
        state[h] = dot(kh, vh, 0, 0)

    @pl.when(seq == 0)
    def _():
        for h in range(heads):
            pre_recv[h] = jnp.zeros((DH, DH), bf16)
            pre_send[h] = state[h].astype(bf16)

    greeted = (n_sub - 1) + (n_head - 1)
    around = jnp.where(seq > 0, 1, 0) + jnp.where(seq < n_seq - 1, 1, 0)
    pl.semaphore_wait(barrier, greeted + around)

    def pre_copy(h):
        return pltpu.make_async_remote_copy(
            src_ref=pre_send.at[h],
            dst_ref=pre_recv.at[h],
            send_sem=pre_ssem.at[h],
            recv_sem=pre_rsem.at[h],
            device_id={"seq": seq + 1},
            device_id_type=MESH,
        )

    @pl.when(jnp.logical_and(seq == 0, seq < n_seq - 1))
    def _():
        for h in range(heads):
            pre_copy(h).start()

    sib_copies = []
    for d in list(range(1, n_head)) + [0]:
        for e in range(1, n_sub):
            other = lax.rem(sub + e, n_sub)
            copy = pltpu.make_async_remote_copy(
                src_ref=w_hbm.at[:, block_of(d, other)],
                dst_ref=w_sib.at[e - 1, d],
                send_sem=ws_send.at[e - 1, d],
                recv_sem=ws_recv.at[e - 1, d],
                device_id={"sub": other},
                device_id_type=MESH,
            )
            copy.start()
            sib_copies.append(copy)
    for d in list(range(1, n_head)) + [0]:
        own_loads[d].start()

    for i in range(2, 6):
        loads[i].wait()

    ctx_mask = (
        lax.broadcasted_iota(jnp.int32, (rows, rows), 0)
        >= lax.broadcasted_iota(jnp.int32, (rows, rows), 1)
    )
    opt_masks = []
    for o in range(opts):
        col = lax.broadcasted_iota(jnp.int32, (slots, total), 1)
        row = lax.broadcasted_iota(jnp.int32, (slots, total), 0)
        first = rows + o * slots
        here = jnp.logical_and(col >= first, col <= row + first)
        opt_masks.append(jnp.logical_or(col < jnp.minimum(offs[o], rows), here))
    for h in range(heads):
        qh = q_buf[:, head_cols(h)].astype(bf16)
        kh = k_buf[:, head_cols(h)].astype(bf16)
        vh = v_buf[:, head_cols(h)].astype(bf16)
        scores = jnp.where(ctx_mask, dot(qh[:rows], kh[:rows], 1, 1), 0.0)
        intra[h, :rows] = dot(scores.astype(bf16), vh[:rows], 1, 0)
        opt_scores = dot(qh[rows:], kh, 1, 1)
        opt_scores = jnp.concatenate([
            jnp.where(opt_masks[o], opt_scores[o * slots:(o + 1) * slots], 0.0)
            for o in range(opts)
        ])
        intra[h, rows:] = dot(opt_scores.astype(bf16), vh, 1, 0)

    slot = lax.broadcasted_iota(jnp.int32, (slots, DH), 0)
    valid = [jnp.where(slot < lens[o], 1.0, 0.0) for o in range(opts)]

    n_copies = []
    for h in range(heads):
        @pl.when(seq > 0)
        def _():
            pre_copy(h).wait_recv()

            @pl.when(seq < n_seq - 1)
            def _():
                pre_send[h] = (state[h] + pre_recv[h].astype(f32)).astype(bf16)
                pre_copy(h).start()

        qh = q_buf[:, head_cols(h)].astype(bf16)
        att = intra[h] + dot(qh, pre_recv[h], 1, 0)
        square = jnp.mean(att * att, axis=-1, keepdims=True)
        out = att * lax.rsqrt(square + norm_epsilon) * gain_ref[:, head_cols(h)]
        normed[:rows, head_cols(h)] = out[:rows].astype(bf16)
        for o in range(opts):
            at = slice(rows + o * slots, rows + (o + 1) * slots)
            normed[at, head_cols(h)] = (out[at] * valid[o]).astype(bf16)
        for e in range(1, n_sub):
            copy = pltpu.make_async_remote_copy(
                src_ref=normed.at[:, pl.ds(h * DH, DH)],
                dst_ref=sib_normed.at[e - 1, :, pl.ds(h * DH, DH)],
                send_sem=n_send.at[e - 1, h],
                recv_sem=n_recv.at[e - 1, h],
                device_id={"sub": lax.rem(sub + e, n_sub)},
                device_id_type=MESH,
            )
            copy.start()
            n_copies.append(copy)

    for d in range(n_head):
        own_loads[d].wait()
    for copy in sib_copies:
        copy.wait_recv()
    for copy in n_copies:
        copy.wait_recv()

    def project(d, c):
        at = pl.ds(c * width, width)
        result = dot(normed[...], w_own[d, :, at], 1, 0)
        for e in range(n_sub - 1):
            result = result + dot(sib_normed[e], w_sib[e, d, :, at], 1, 0)
        return result

    x_copies = {}
    for c in range(chunks):
        for d in range(1, n_head):
            part_send[d - 1, c] = project(d, c).astype(bf16)
            copy = pltpu.make_async_remote_copy(
                src_ref=part_send.at[d - 1, c],
                dst_ref=part_recv.at[d - 1, c],
                send_sem=x_send.at[d - 1, c],
                recv_sem=x_recv.at[d - 1, c],
                device_id={"head": lax.rem(head + d, n_head)},
                device_id_type=MESH,
            )
            copy.start()
            x_copies[d, c] = copy
    for c in range(chunks):
        own_part[c] = project(0, c)
    for c in range(chunks):
        result = own_part[c]
        for d in range(1, n_head):
            x_copies[d, c].wait_recv()
            result = result + part_recv[d - 1, c].astype(f32)
        at = slice(c * width, (c + 1) * width)
        ctx_out[:, at] = result[:rows].astype(bf16)
        opt_out[:, at] = result[rows:].astype(bf16)

    for copy in list(x_copies.values()) + n_copies + sib_copies:
        copy.wait_send()

    @pl.when(seq < n_seq - 1)
    def _():
        for h in range(heads):
            pre_copy(h).wait_send()


def on_device(
    queries, keys, values, opt_queries, opt_keys, opt_values,
    opt_offsets, opt_lengths, norm_gain, out_weight,
):
    n_seq, n_head, n_sub = (lax.axis_size(a) for a in ("seq", "head", "sub"))
    rows, features = queries.shape
    opts, slots, _ = opt_queries.shape
    heads = features // DH
    total = rows + opts * slots
    columns = out_weight.shape[1] // (n_head * n_sub)
    width = 256 if columns % 256 == 0 else columns
    chunks = columns // width
    flat = lambda a: a.reshape(opts * slots, features)
    anyspace = pl.BlockSpec(memory_space=pl.ANY)
    vmem = pl.BlockSpec(memory_space=pltpu.VMEM)
    smem = pl.BlockSpec(memory_space=pltpu.SMEM)
    sem = pltpu.SemaphoreType.DMA
    ctx, opt = pl.pallas_call(
        functools.partial(kernel, (n_seq, n_head, n_sub, rows, opts, slots, chunks)),
        out_shape=(
            jax.ShapeDtypeStruct((rows, columns), bf16),
            jax.ShapeDtypeStruct((opts * slots, columns), bf16),
        ),
        in_specs=[anyspace] * 6 + [smem, smem, vmem, anyspace],
        out_specs=(vmem, vmem),
        scratch_shapes=[
            pltpu.VMEM((total, features), f32),
            pltpu.VMEM((total, features), f32),
            pltpu.VMEM((total, features), f32),
            pltpu.VMEM((heads, DH, DH), f32),
            pltpu.VMEM((heads, total, DH), f32),
            pltpu.VMEM((heads, DH, DH), bf16),
            pltpu.VMEM((heads, DH, DH), bf16),
            pltpu.VMEM((total, features), bf16),
            pltpu.VMEM((n_sub - 1, total, features), bf16),
            pltpu.VMEM((n_head, features, columns), bf16),
            pltpu.VMEM((n_sub - 1, n_head, features, columns), bf16),
            pltpu.VMEM((n_head - 1, chunks, total, width), bf16),
            pltpu.VMEM((n_head - 1, chunks, total, width), bf16),
            pltpu.VMEM((chunks, total, width), f32),
            sem((6,)),
            sem((n_head,)),
            sem((n_sub - 1, n_head)),
            sem((n_sub - 1, n_head)),
            sem((heads,)),
            sem((heads,)),
            sem((n_sub - 1, heads)),
            sem((n_sub - 1, heads)),
            sem((n_head - 1, chunks)),
            sem((n_head - 1, chunks)),
        ],
        compiler_params=pltpu.CompilerParams(collective_id=0, has_side_effects=True),
        name="scoring",
    )(
        queries, keys, values, flat(opt_queries), flat(opt_keys), flat(opt_values),
        opt_offsets, opt_lengths, norm_gain.reshape(1, features), out_weight,
    )
    return ctx, opt.reshape(opts, slots, columns)


def solution(mesh):
    placed = (
        P(("grp", "seq"), ("head", "sub")),
        P(("grp", "seq"), ("head", "sub")),
        P(("grp", "seq"), ("head", "sub")),
        P(("grp", "seq"), None, ("head", "sub")),
        P(("grp", "seq"), None, ("head", "sub")),
        P(("grp", "seq"), None, ("head", "sub")),
        P(("grp", "seq")),
        P(("grp", "seq")),
        P(("head", "sub")),
        P(("head", "sub"), None),
    )
    return jax.shard_map(
        on_device,
        mesh=mesh,
        in_specs=placed,
        out_specs=(P(("grp", "seq"), ("head", "sub")), P(("grp", "seq"), None, ("head", "sub"))),
        check_vma=False,
    )
```

time: 92 us -> 34.2 us (0.37)
  blocking collectives: 54.9 us -> 0 us
  Pallas kernels: 0 us -> 29.8 us
  matrix products: 13.1 us -> 0 us
  local copies, waits for them, and re-layouts: 14.1 us -> 3.44 us
  starting transfers between devices: 5.6 us -> 0 us
  other arithmetic: 2.7 us -> 0 us
    all_gather x3 -> x0, blocking collectives: 54.9 us -> none  [the longest x1 33.1 us: on_device(): lax.all_gather(opt_normed, ('head', 'sub'), axis=1, tiled=True)]
    pallas_call x0 -> x1, Pallas kernels: none -> 29.8 us  [on_device(): pl.pallas_call(functools.partial(kernel, (n_seq, n_head, n_sub, rows, opt...]
    dot_general x10 -> x0, matrix products: 13.1 us -> none  [the longest x2 6.22 us: grouped_project(): jnp.einsum('rgk,gkd->grd', flat, weight_groups, preferred_element_type=jn...]
    all_to_all x1 -> x0, local copies, waits for them, and re-layouts: 6.33 us -> none  [on_device(): lax.all_to_all(out_weight, ('head', 'sub'), split_axis=1, concat_axis=0,...]
    all_to_all x1 -> x0, starting transfers between devices: 5.6 us -> none  [on_device(): lax.all_to_all(out_weight, ('head', 'sub'), split_axis=1, concat_axis=0,...]
    unnamed x22 -> x2, local copies, waits for them, and re-layouts: 6.6 us -> 3.44 us
    reduce_sum x2 -> x0, other arithmetic: 2.06 us -> none  [grouped_project(): return jnp.sum(partial_value, axis=0).astype(jnp.bfloat16)]
    all_gather x1 -> x0, local copies, waits for them, and re-layouts: 1.04 us -> none  [on_device(): lax.all_gather(opt_normed, ('head', 'sub'), axis=1, tiled=True)]
  transfers between devices with their start and end apart: 1 -> 0, of which waited for: 0 -> 0; matrix products, arithmetic and copies ran while one was open for 10% -> 0% of each run, Pallas kernels for 0% -> 0%
where the time goes in v1:
time: 34.2 us; the launch traced here: 33.9 us
  Pallas kernels  29.8 us (87%)
  local copies, waits for them, and re-layouts  3.44 us (10%)
  between operations  0.64 us (2%)
    pallas_call x1, Pallas kernels, on_device(): pl.pallas_call(functools.partial(kernel, (n_seq, n_head, n_sub, rows, opt...  29.8 us
    unnamed x2, local copies, waits for them, and re-layouts  3.44 us

profile of v1, /device:TPU:25, one launch (start us, length us, event | category | flops | bytes accessed | tf_op | source)
XLA Modules:
  0.0 33.9 jit_solution(4015319304872723920)
XLA Ops:
  0.6 29.8 %scoring.1 = (bf16[192,1024]{1,0:T(8,128)(2,1)}, bf16[128,1024]{1,0:T(8,128)(2,1)}) custom-call(f32[192,512]{1,0:T(8,128)} %q_hbm.1, f32[192,512]{1,0:T(8,128)} %k_hbm.1, f32[192,512]{1,0:T(8,128)} %v_hbm.1, f32[128,512]{1,0:T(8,128)} %bitcast.5, f32[128,512]{1,0:T(8,128)} %bitcast.6, f32[128,512]{1,0:T(8,128)} %bitcast.7, s32[2]{0:T(128)} %offs.1, s32[2]{0:T(128)} %lens.1, ...), custom_call_target="tpu_custom_call" | custom-call | tf_op jit(solution)/shard_map/scoring/pallas_call | solution.py:257
  30.5 1.8 %copy.14 = bf16[192,1024]{1,0:T(8,128)(2,1)} copy(bf16[192,1024]{1,0:T(8,128)(2,1)} %get-tuple-element.8) | data formatting | bytes 786432
  32.2 1.7 %copy.15 = bf16[2,64,1024]{2,1,0:T(8,128)(2,1)} copy(bf16[2,64,1024]{2,1,0:T(8,128)(2,1)} %bitcast.8) | data formatting | bytes 524288

commit v2 on v1

--- a/solution.py
+++ b/solution.py
@@ -142,6 +142,14 @@
         first = rows + o * slots
         here = jnp.logical_and(col >= first, col <= row + first)
         opt_masks.append(jnp.logical_or(col < jnp.minimum(offs[o], rows), here))
+    def relay(h):
+        pre_copy(h).wait_recv()
+
+        @pl.when(seq < n_seq - 1)
+        def _():
+            pre_send[h] = (state[h] + pre_recv[h].astype(f32)).astype(bf16)
+            pre_copy(h).start()
+
     for h in range(heads):
         qh = q_buf[:, head_cols(h)].astype(bf16)
         kh = k_buf[:, head_cols(h)].astype(bf16)
@@ -155,19 +163,18 @@
         ])
         intra[h, rows:] = dot(opt_scores.astype(bf16), vh, 1, 0)
 
+        @pl.when(seq == 1)
+        def _():
+            relay(h)
+
     slot = lax.broadcasted_iota(jnp.int32, (slots, DH), 0)
     valid = [jnp.where(slot < lens[o], 1.0, 0.0) for o in range(opts)]
 
     n_copies = []
     for h in range(heads):
-        @pl.when(seq > 0)
+        @pl.when(seq > 1)
         def _():
-            pre_copy(h).wait_recv()
-
-            @pl.when(seq < n_seq - 1)
-            def _():
-                pre_send[h] = (state[h] + pre_recv[h].astype(f32)).astype(bf16)
-                pre_copy(h).start()
+            relay(h)
 
         qh = q_buf[:, head_cols(h)].astype(bf16)
         att = intra[h] + dot(qh, pre_recv[h], 1, 0)
@@ -237,6 +244,17 @@
             pre_copy(h).wait_send()
 
 
+def write_out(ctx, opt, ctx_hbm, opt_hbm, out_sem):
+    copies = [
+        pltpu.make_async_copy(ctx, ctx_hbm, out_sem.at[0]),
+        pltpu.make_async_copy(opt, opt_hbm, out_sem.at[1]),
+    ]
+    for copy in copies:
+        copy.start()
+    for copy in copies:
+        copy.wait()
+
+
 def on_device(
     queries, keys, values, opt_queries, opt_keys, opt_values,
     opt_offsets, opt_lengths, norm_gain, out_weight,
@@ -257,8 +275,8 @@
     ctx, opt = pl.pallas_call(
         functools.partial(kernel, (n_seq, n_head, n_sub, rows, opts, slots, chunks)),
         out_shape=(
-            jax.ShapeDtypeStruct((rows, columns), bf16),
-            jax.ShapeDtypeStruct((opts * slots, columns), bf16),
+            pltpu.VMEM((rows, columns), bf16),
+            pltpu.VMEM((opts * slots, columns), bf16),
         ),
         in_specs=[anyspace] * 6 + [smem, smem, vmem, anyspace],
         out_specs=(vmem, vmem),
@@ -294,6 +312,18 @@
         queries, keys, values, flat(opt_queries), flat(opt_keys), flat(opt_values),
         opt_offsets, opt_lengths, norm_gain.reshape(1, features), out_weight,
     )
+    ctx, opt = pl.pallas_call(
+        write_out,
+        out_shape=(
+            jax.ShapeDtypeStruct((rows, columns), bf16),
+            jax.ShapeDtypeStruct((opts * slots, columns), bf16),
+        ),
+        in_specs=[anyspace, anyspace],
+        out_specs=(anyspace, anyspace),
+        scratch_shapes=[sem((2,))],
+        compiler_params=pltpu.CompilerParams(vmem_limit_bytes=1 << 20),
+        name="write_out",
+    )(ctx, opt)
     return ctx, opt.reshape(opts, slots, columns)
 
 

time: 34.2 us -> 31.1 us (0.909)
  local copies, waits for them, and re-layouts: 3.44 us -> 0 us
  Pallas kernels: 29.8 us -> 30.3 us
    unnamed x2 -> x0, local copies, waits for them, and re-layouts: 3.44 us -> none
    pallas_call x0 -> x1, Pallas kernels: none -> 0.85 us  [on_device(): pl.pallas_call(write_out, out_shape=(jax.ShapeDtypeStruct((rows, columns)...]
    pallas_call x1, Pallas kernels: 29.8 us -> 29.4 us  [on_device(): pl.pallas_call(functools.partial(kernel, (n_seq, n_head, n_sub, rows, opt...]
where the time goes in v2:
time: 31.1 us; the launch traced here: 30.9 us
  Pallas kernels  30.3 us (97%)
  between operations  0.64 us (2%)
    pallas_call x1, Pallas kernels, on_device(): pl.pallas_call(functools.partial(kernel, (n_seq, n_head, n_sub, rows, opt...  29.4 us
    pallas_call x1, Pallas kernels, on_device(): pl.pallas_call(write_out, out_shape=(jax.ShapeDtypeStruct((rows, columns)...  0.85 us

profile of v2, /device:TPU:25, one launch (start us, length us, event | category | flops | bytes accessed | tf_op | source)
XLA Modules:
  0.0 30.9 jit_solution(5211213083330134721)
XLA Ops:
  0.6 29.4 %scoring.1 = (bf16[192,1024]{1,0:T(8,128)(2,1)S(1)}, bf16[128,1024]{1,0:T(8,128)(2,1)S(1)}) custom-call(f32[192,512]{1,0:T(8,128)} %q_hbm.1, f32[192,512]{1,0:T(8,128)} %k_hbm.1, f32[192,512]{1,0:T(8,128)} %v_hbm.1, f32[128,512]{1,0:T(8,128)} %bitcast.5, f32[128,512]{1,0:T(8,128)} %bitcast.6, f32[128,512]{1,0:T(8,128)} %bitcast.7, s32[2]{0:T(128)} %offs.1, ...), custom_call_target="tpu_custom_call" | custom-call | tf_op jit(solution)/shard_map/scoring/pallas_call | solution.py:275
  30.0 0.9 %write_out.1 = (bf16[192,1024]{1,0:T(8,128)(2,1)}, bf16[128,1024]{1,0:T(8,128)(2,1)}) custom-call(bf16[192,1024]{1,0:T(8,128)(2,1)S(1)} %get-tuple-element.6.ctx, bf16[128,1024]{1,0:T(8,128)(2,1)S(1)} %get-tuple-element.7.opt), custom_call_target="tpu_custom_call" | custom-call | tf_op jit(solution)/shard_map/write_out/pallas_call | solution.py:315

commit v3 on v2

--- a/solution.py
+++ b/solution.py
@@ -8,6 +8,8 @@
 from jax.sharding import PartitionSpec as P
 
 DH = 128
+PIECES = 2
+PIECE = DH // PIECES
 norm_epsilon = 1e-05
 MESH = pl.DeviceIdType.MESH
 bf16 = jnp.bfloat16
@@ -20,10 +22,11 @@
 
 def kernel(
     sizes,
-    q_hbm, k_hbm, v_hbm, oq_hbm, ok_hbm, ov_hbm, offs, lens, gain_ref, w_hbm,
+    q_hbm, k_hbm, v_hbm, oq_hbm, ok_hbm, ov_hbm, offs_hbm, lens_hbm, gain_hbm, w_hbm,
     ctx_out, opt_out,
     q_buf, k_buf, v_buf, state, intra, pre_recv, pre_send, normed, sib_normed,
     w_own, w_sib, part_send, part_recv, own_part,
+    offs, lens, gain_ref,
     in_sem, w_sem, ws_send, ws_recv, pre_ssem, pre_rsem, n_send, n_recv, x_send, x_recv,
 ):
     n_seq, n_head, n_sub, rows, opts, slots, chunks = sizes
@@ -66,6 +69,10 @@
         copy = pltpu.make_async_copy(src, dst.at[pl.ds(at, count)], in_sem.at[i])
         copy.start()
         loads.append(copy)
+    for i, (src, dst) in enumerate(((offs_hbm, offs), (lens_hbm, lens), (gain_hbm, gain_ref))):
+        copy = pltpu.make_async_copy(src, dst, in_sem.at[6 + i])
+        copy.start()
+        loads.append(copy)
 
     def block_of(d, s):
         place = lax.rem(head + d, n_head) * n_sub + s
@@ -96,12 +103,12 @@
     around = jnp.where(seq > 0, 1, 0) + jnp.where(seq < n_seq - 1, 1, 0)
     pl.semaphore_wait(barrier, greeted + around)
 
-    def pre_copy(h):
+    def pre_copy(h, p):
         return pltpu.make_async_remote_copy(
-            src_ref=pre_send.at[h],
-            dst_ref=pre_recv.at[h],
-            send_sem=pre_ssem.at[h],
-            recv_sem=pre_rsem.at[h],
+            src_ref=pre_send.at[h, pl.ds(p * PIECE, PIECE)],
+            dst_ref=pre_recv.at[h, pl.ds(p * PIECE, PIECE)],
+            send_sem=pre_ssem.at[h, p],
+            recv_sem=pre_rsem.at[h, p],
             device_id={"seq": seq + 1},
             device_id_type=MESH,
         )
@@ -109,7 +116,8 @@
     @pl.when(jnp.logical_and(seq == 0, seq < n_seq - 1))
     def _():
         for h in range(heads):
-            pre_copy(h).start()
+            for p in range(PIECES):
+                pre_copy(h, p).start()
 
     sib_copies = []
     for d in list(range(1, n_head)) + [0]:
@@ -128,7 +136,7 @@
     for d in list(range(1, n_head)) + [0]:
         own_loads[d].start()
 
-    for i in range(2, 6):
+    for i in range(2, 9):
         loads[i].wait()
 
     ctx_mask = (
@@ -143,12 +151,14 @@
         here = jnp.logical_and(col >= first, col <= row + first)
         opt_masks.append(jnp.logical_or(col < jnp.minimum(offs[o], rows), here))
     def relay(h):
-        pre_copy(h).wait_recv()
-
-        @pl.when(seq < n_seq - 1)
-        def _():
-            pre_send[h] = (state[h] + pre_recv[h].astype(f32)).astype(bf16)
-            pre_copy(h).start()
+        for p in range(PIECES):
+            pre_copy(h, p).wait_recv()
+
+            @pl.when(seq < n_seq - 1)
+            def _():
+                at = slice(p * PIECE, (p + 1) * PIECE)
+                pre_send[h, at] = (state[h, at] + pre_recv[h, at].astype(f32)).astype(bf16)
+                pre_copy(h, p).start()
 
     for h in range(heads):
         qh = q_buf[:, head_cols(h)].astype(bf16)
@@ -241,7 +251,8 @@
     @pl.when(seq < n_seq - 1)
     def _():
         for h in range(heads):
-            pre_copy(h).wait_send()
+            for p in range(PIECES):
+                pre_copy(h, p).wait_send()
 
 
 def write_out(ctx, opt, ctx_hbm, opt_hbm, out_sem):
@@ -270,7 +281,6 @@
     flat = lambda a: a.reshape(opts * slots, features)
     anyspace = pl.BlockSpec(memory_space=pl.ANY)
     vmem = pl.BlockSpec(memory_space=pltpu.VMEM)
-    smem = pl.BlockSpec(memory_space=pltpu.SMEM)
     sem = pltpu.SemaphoreType.DMA
     ctx, opt = pl.pallas_call(
         functools.partial(kernel, (n_seq, n_head, n_sub, rows, opts, slots, chunks)),
@@ -278,7 +288,7 @@
             pltpu.VMEM((rows, columns), bf16),
             pltpu.VMEM((opts * slots, columns), bf16),
         ),
-        in_specs=[anyspace] * 6 + [smem, smem, vmem, anyspace],
+        in_specs=[anyspace] * 10,
         out_specs=(vmem, vmem),
         scratch_shapes=[
             pltpu.VMEM((total, features), f32),
@@ -295,12 +305,15 @@
             pltpu.VMEM((n_head - 1, chunks, total, width), bf16),
             pltpu.VMEM((n_head - 1, chunks, total, width), bf16),
             pltpu.VMEM((chunks, total, width), f32),
-            sem((6,)),
+            pltpu.SMEM((opts,), jnp.int32),
+            pltpu.SMEM((opts,), jnp.int32),
+            pltpu.VMEM((1, features), f32),
+            sem((9,)),
             sem((n_head,)),
             sem((n_sub - 1, n_head)),
             sem((n_sub - 1, n_head)),
-            sem((heads,)),
-            sem((heads,)),
+            sem((heads, PIECES)),
+            sem((heads, PIECES)),
             sem((n_sub - 1, heads)),
             sem((n_sub - 1, heads)),
             sem((n_head - 1, chunks)),

time: 31.1 us -> 30.3 us (0.974)
  Pallas kernels: 30.3 us -> 29.5 us
    pallas_call x1, Pallas kernels: 29.4 us -> 28.6 us  [on_device(): pl.pallas_call(functools.partial(kernel, (n_seq, n_head, n_sub, rows, opt...]
where the time goes in v3:
time: 30.3 us; the launch traced here: 30.1 us
  Pallas kernels  29.5 us (97%)
  between operations  0.64 us (2%)
    pallas_call x1, Pallas kernels, on_device(): pl.pallas_call(functools.partial(kernel, (n_seq, n_head, n_sub, rows, opt...  28.6 us
    pallas_call x1, Pallas kernels, on_device(): pl.pallas_call(write_out, out_shape=(jax.ShapeDtypeStruct((rows, columns)...  0.85 us

profile of v3, /device:TPU:25, one launch (start us, length us, event | category | flops | bytes accessed | tf_op | source)
XLA Modules:
  0.0 30.1 jit_solution(15438627832860287626)
XLA Ops:
  0.6 28.6 %scoring.1 = (bf16[192,1024]{1,0:T(8,128)(2,1)S(1)}, bf16[128,1024]{1,0:T(8,128)(2,1)S(1)}) custom-call(f32[192,512]{1,0:T(8,128)} %q_hbm.1, f32[192,512]{1,0:T(8,128)} %k_hbm.1, f32[192,512]{1,0:T(8,128)} %v_hbm.1, f32[128,512]{1,0:T(8,128)} %bitcast.5, f32[128,512]{1,0:T(8,128)} %bitcast.6, f32[128,512]{1,0:T(8,128)} %bitcast.7, s32[2]{0:T(128)} %offs_hbm.1, ...), custom_call_target="tpu_custom_call" | custom-call | tf_op jit(solution)/shard_map/scoring/pallas_call | solution.py:285
  29.3 0.9 %write_out.1 = (bf16[192,1024]{1,0:T(8,128)(2,1)}, bf16[128,1024]{1,0:T(8,128)(2,1)}) custom-call(bf16[192,1024]{1,0:T(8,128)(2,1)S(1)} %get-tuple-element.6.ctx, bf16[128,1024]{1,0:T(8,128)(2,1)S(1)} %get-tuple-element.7.opt), custom_call_target="tpu_custom_call" | custom-call | tf_op jit(solution)/shard_map/write_out/pallas_call | solution.py:328

commit v4 on v3

--- a/solution.py
+++ b/solution.py
@@ -210,14 +210,24 @@
         own_loads[d].wait()
     for copy in sib_copies:
         copy.wait_recv()
-    for copy in n_copies:
-        copy.wait_recv()
+    half = max(heads // 2, 1)
+    arrived = set()
+
+    def wait_heads(first, last):
+        for copy_h in range(first, last):
+            for e in range(n_sub - 1):
+                if (copy_h, e) not in arrived:
+                    arrived.add((copy_h, e))
+                    n_copies[copy_h * (n_sub - 1) + e].wait_recv()
 
     def project(d, c):
         at = pl.ds(c * width, width)
         result = dot(normed[...], w_own[d, :, at], 1, 0)
-        for e in range(n_sub - 1):
-            result = result + dot(sib_normed[e], w_sib[e, d, :, at], 1, 0)
+        for first, last in ((0, half), (half, heads)):
+            wait_heads(first, last)
+            part = slice(first * DH, last * DH)
+            for e in range(n_sub - 1):
+                result = result + dot(sib_normed[e, :, part], w_sib[e, d, part, at], 1, 0)
         return result
 
     x_copies = {}

time: 30.3 us -> 30.4 us (level)
  no operation moved by 1% of the time
where the time goes in v4:
time: 30.4 us; the launch traced here: 30.3 us
  Pallas kernels  29.6 us (97%)
  between operations  0.64 us (2%)
    pallas_call x1, Pallas kernels, on_device(): pl.pallas_call(functools.partial(kernel, (n_seq, n_head, n_sub, rows, opt...  28.8 us
    pallas_call x1, Pallas kernels, on_device(): pl.pallas_call(write_out, out_shape=(jax.ShapeDtypeStruct((rows, columns)...  0.85 us

profile of v4, /device:TPU:25, one launch (start us, length us, event | category | flops | bytes accessed | tf_op | source)
XLA Modules:
  0.0 30.3 jit_solution(2351870667639299733)
XLA Ops:
  0.6 28.8 %scoring.1 = (bf16[192,1024]{1,0:T(8,128)(2,1)S(1)}, bf16[128,1024]{1,0:T(8,128)(2,1)S(1)}) custom-call(f32[192,512]{1,0:T(8,128)} %q_hbm.1, f32[192,512]{1,0:T(8,128)} %k_hbm.1, f32[192,512]{1,0:T(8,128)} %v_hbm.1, f32[128,512]{1,0:T(8,128)} %bitcast.5, f32[128,512]{1,0:T(8,128)} %bitcast.6, f32[128,512]{1,0:T(8,128)} %bitcast.7, s32[2]{0:T(128)} %offs_hbm.1, ...), custom_call_target="tpu_custom_call" | custom-call | tf_op jit(solution)/shard_map/scoring/pallas_call | solution.py:295
  29.4 0.9 %write_out.1 = (bf16[192,1024]{1,0:T(8,128)(2,1)}, bf16[128,1024]{1,0:T(8,128)(2,1)}) custom-call(bf16[192,1024]{1,0:T(8,128)(2,1)S(1)} %get-tuple-element.6.ctx, bf16[128,1024]{1,0:T(8,128)(2,1)S(1)} %get-tuple-element.7.opt), custom_call_target="tpu_custom_call" | custom-call | tf_op jit(solution)/shard_map/write_out/pallas_call | solution.py:338

commit v5 on v4

--- a/solution.py
+++ b/solution.py
@@ -120,7 +120,8 @@
                 pre_copy(h, p).start()
 
     sib_copies = []
-    for d in list(range(1, n_head)) + [0]:
+
+    def fetch(d):
         for e in range(1, n_sub):
             other = lax.rem(sub + e, n_sub)
             copy = pltpu.make_async_remote_copy(
@@ -133,8 +134,16 @@
             )
             copy.start()
             sib_copies.append(copy)
-    for d in list(range(1, n_head)) + [0]:
         own_loads[d].start()
+
+    def fetched(d):
+        own_loads[d].wait()
+        at = (n_head - 1 if d == 0 else d - 1) * (n_sub - 1)
+        for copy in sib_copies[at:at + n_sub - 1]:
+            copy.wait_recv()
+
+    for d in range(1, n_head):
+        fetch(d)
 
     for i in range(2, 9):
         loads[i].wait()
@@ -206,10 +215,8 @@
             copy.start()
             n_copies.append(copy)
 
-    for d in range(n_head):
-        own_loads[d].wait()
-    for copy in sib_copies:
-        copy.wait_recv()
+    for d in range(1, n_head):
+        fetched(d)
     half = max(heads // 2, 1)
     arrived = set()
 
@@ -244,6 +251,8 @@
             )
             copy.start()
             x_copies[d, c] = copy
+    fetch(0)
+    fetched(0)
     for c in range(chunks):
         own_part[c] = project(0, c)
     for c in range(chunks):

time: 30.4 us -> 30.4 us (level)
  no operation moved by 1% of the time
where the time goes in v5:
time: 30.4 us; the launch traced here: 30.3 us
  Pallas kernels  29.6 us (97%)
  between operations  0.64 us (2%)
    pallas_call x1, Pallas kernels, on_device(): pl.pallas_call(functools.partial(kernel, (n_seq, n_head, n_sub, rows, opt...  28.8 us
    pallas_call x1, Pallas kernels, on_device(): pl.pallas_call(write_out, out_shape=(jax.ShapeDtypeStruct((rows, columns)...  0.85 us

profile of v5, /device:TPU:25, one launch (start us, length us, event | category | flops | bytes accessed | tf_op | source)
XLA Modules:
  0.0 30.3 jit_solution(15443738861644562311)
XLA Ops:
  0.6 28.8 %scoring.1 = (bf16[192,1024]{1,0:T(8,128)(2,1)S(1)}, bf16[128,1024]{1,0:T(8,128)(2,1)S(1)}) custom-call(f32[192,512]{1,0:T(8,128)} %q_hbm.1, f32[192,512]{1,0:T(8,128)} %k_hbm.1, f32[192,512]{1,0:T(8,128)} %v_hbm.1, f32[128,512]{1,0:T(8,128)} %bitcast.5, f32[128,512]{1,0:T(8,128)} %bitcast.6, f32[128,512]{1,0:T(8,128)} %bitcast.7, s32[2]{0:T(128)} %offs_hbm.1, ...), custom_call_target="tpu_custom_call" | custom-call | tf_op jit(solution)/shard_map/scoring/pallas_call | solution.py:304
  29.4 0.9 %write_out.1 = (bf16[192,1024]{1,0:T(8,128)(2,1)}, bf16[128,1024]{1,0:T(8,128)(2,1)}) custom-call(bf16[192,1024]{1,0:T(8,128)(2,1)S(1)} %get-tuple-element.6.ctx, bf16[128,1024]{1,0:T(8,128)(2,1)S(1)} %get-tuple-element.7.opt), custom_call_target="tpu_custom_call" | custom-call | tf_op jit(solution)/shard_map/write_out/pallas_call | solution.py:347

commit v6 on v5

--- a/solution.py
+++ b/solution.py
@@ -8,7 +8,7 @@
 from jax.sharding import PartitionSpec as P
 
 DH = 128
-PIECES = 2
+PIECES = 4
 PIECE = DH // PIECES
 norm_epsilon = 1e-05
 MESH = pl.DeviceIdType.MESH

time: 30.4 us -> 30.5 us (level)
  no operation moved by 1% of the time
where the time goes in v6:
time: 30.5 us; the launch traced here: 30.4 us
  Pallas kernels  29.7 us (97%)
  between operations  0.64 us (2%)
    pallas_call x1, Pallas kernels, on_device(): pl.pallas_call(functools.partial(kernel, (n_seq, n_head, n_sub, rows, opt...  28.9 us
    pallas_call x1, Pallas kernels, on_device(): pl.pallas_call(write_out, out_shape=(jax.ShapeDtypeStruct((rows, columns)...  0.85 us

profile of v6, /device:TPU:25, one launch (start us, length us, event | category | flops | bytes accessed | tf_op | source)
XLA Modules:
  0.0 30.4 jit_solution(12029995662715448057)
XLA Ops:
  0.6 28.9 %scoring.1 = (bf16[192,1024]{1,0:T(8,128)(2,1)S(1)}, bf16[128,1024]{1,0:T(8,128)(2,1)S(1)}) custom-call(f32[192,512]{1,0:T(8,128)} %q_hbm.1, f32[192,512]{1,0:T(8,128)} %k_hbm.1, f32[192,512]{1,0:T(8,128)} %v_hbm.1, f32[128,512]{1,0:T(8,128)} %bitcast.5, f32[128,512]{1,0:T(8,128)} %bitcast.6, f32[128,512]{1,0:T(8,128)} %bitcast.7, s32[2]{0:T(128)} %offs_hbm.1, ...), custom_call_target="tpu_custom_call" | custom-call | tf_op jit(solution)/shard_map/scoring/pallas_call | solution.py:304
  29.5 0.9 %write_out.1 = (bf16[192,1024]{1,0:T(8,128)(2,1)}, bf16[128,1024]{1,0:T(8,128)(2,1)}) custom-call(bf16[192,1024]{1,0:T(8,128)(2,1)S(1)} %get-tuple-element.6.ctx, bf16[128,1024]{1,0:T(8,128)(2,1)S(1)} %get-tuple-element.7.opt), custom_call_target="tpu_custom_call" | custom-call | tf_op jit(solution)/shard_map/write_out/pallas_call | solution.py:347

commit v7 on v4

--- a/solution.py
+++ b/solution.py
@@ -286,7 +286,7 @@
     heads = features // DH
     total = rows + opts * slots
     columns = out_weight.shape[1] // (n_head * n_sub)
-    width = 256 if columns % 256 == 0 else columns
+    width = 128 if columns % 128 == 0 else columns
     chunks = columns // width
     flat = lambda a: a.reshape(opts * slots, features)
     anyspace = pl.BlockSpec(memory_space=pl.ANY)

time: 30.4 us -> 30.5 us (level)
  no operation moved by 1% of the time
where the time goes in v7:
time: 30.5 us; the launch traced here: 30.3 us
  Pallas kernels  29.7 us (97%)
  between operations  0.64 us (2%)
    pallas_call x1, Pallas kernels, on_device(): pl.pallas_call(functools.partial(kernel, (n_seq, n_head, n_sub, rows, opt...  28.9 us
    pallas_call x1, Pallas kernels, on_device(): pl.pallas_call(write_out, out_shape=(jax.ShapeDtypeStruct((rows, columns)...  0.85 us

profile of v7, /device:TPU:25, one launch (start us, length us, event | category | flops | bytes accessed | tf_op | source)
XLA Modules:
  0.0 30.3 jit_solution(2570545122576899634)
XLA Ops:
  0.6 28.9 %scoring.1 = (bf16[192,1024]{1,0:T(8,128)(2,1)S(1)}, bf16[128,1024]{1,0:T(8,128)(2,1)S(1)}) custom-call(f32[192,512]{1,0:T(8,128)} %q_hbm.1, f32[192,512]{1,0:T(8,128)} %k_hbm.1, f32[192,512]{1,0:T(8,128)} %v_hbm.1, f32[128,512]{1,0:T(8,128)} %bitcast.5, f32[128,512]{1,0:T(8,128)} %bitcast.6, f32[128,512]{1,0:T(8,128)} %bitcast.7, s32[2]{0:T(128)} %offs_hbm.1, ...), custom_call_target="tpu_custom_call" | custom-call | tf_op jit(solution)/shard_map/scoring/pallas_call | solution.py:295
  29.5 0.9 %write_out.1 = (bf16[192,1024]{1,0:T(8,128)(2,1)}, bf16[128,1024]{1,0:T(8,128)(2,1)}) custom-call(bf16[192,1024]{1,0:T(8,128)(2,1)S(1)} %get-tuple-element.6.ctx, bf16[128,1024]{1,0:T(8,128)(2,1)S(1)} %get-tuple-element.7.opt), custom_call_target="tpu_custom_call" | custom-call | tf_op jit(solution)/shard_map/write_out/pallas_call | solution.py:338
